TPU v7x, 32 devices: a whole 2x2x4 slice. The times are simulated.
32 devices in a mesh: narrow: 4 (over y, x), region: 8 (over z, core).
Axes of the slice: x: 2, y: 2, z: 4, core: 2. Of those that a mesh axis runs over, the one named last changes fastest.
Arguments:
- point_feats: bfloat16 [64, 131072], P(None, ('narrow', 'region')), may hold values from -6 to 6
- point_owner: int32 [131072, 1], P(('narrow', 'region')), may hold values from 0 to 31; in each aligned block of 4096 rows (0 to 4095, 4096 to 8191, ...) at most 256 rows name the same one
- point_voxel: int32 [131072], P(('narrow', 'region')), may hold values from 0 to 12287
- weight: bfloat16 [9, 64, 192], replicated, may hold values from -0.15625 to 0.15625
- cotangent: bfloat16 [64, 192, 2048], P(None, 'region', 'narrow'), may hold values from -6 to 6
Outputs:
- conv_out: bfloat16 [64, 192, 2048], P(None, 'region', 'narrow')
- point_grad: bfloat16 [64, 131072], P(None, ('narrow', 'region'))
- weight_grad: float32 [9, 64, 192], replicated
Inputs may be any that keep to these rules, and one draw needn't show every extreme that they name: `point_owner`: among the 4096 points of one device no owner is named more than 256 times, a bound that some block reaches.
All inputs are finite; a program needn't handle non-finite values.
Results may differ from a plain program's by a relative error of at most 0.0036.
Values may be sent and summed in bfloat16 or wider, within the bound.
A program may use at most 192 MiB of HBM per device.

v0:
```python
import math
import jax
import jax.numpy as jnp
from jax import lax
from jax.sharding import PartitionSpec as P

NZ = 64
CY = 8


def extended(cells, sides, width):
    for axis, dim in sides:
        count = lax.axis_size(axis)
        ends = count - 1
        head = lax.slice_in_dim(cells, 0, width, axis=dim)
        tail = lax.slice_in_dim(cells, cells.shape[dim] - width, cells.shape[dim], axis=dim)
        cells = jnp.concatenate(
            [
                lax.ppermute(tail, axis, [(i, (i + 1) % count) for i in range(ends)]),
                cells,
                lax.ppermute(head, axis, [((i + 1) % count, i) for i in range(ends)]),
            ],
            axis=dim,
        )
    return cells


def stack_depth(padded, offsets, depth):
    return jnp.concatenate([padded[..., o : o + depth] for o in offsets], axis=0)


def shards(point_feats, point_owner, point_voxel, weight, cotangent):
    n_narrow = lax.axis_size("narrow")
    n_region = lax.axis_size("region")
    devices = n_narrow * n_region
    chans, points_here = point_feats.shape
    slots = 2 * points_here // devices
    rows_x = cotangent.shape[1]
    voxels = rows_x * CY * NZ
    owner = point_owner[:, 0]
    marks = (owner[:, None] == jnp.arange(devices, dtype=jnp.int32)[None, :]).astype(jnp.int32)
    slot = jnp.sum(jnp.cumsum(marks, axis=0) * marks, axis=1) - 1
    send_feats = jnp.zeros((devices, slots, chans), jnp.bfloat16).at[owner, slot].set(point_feats.T)
    send_feats = send_feats.reshape(devices, slots * chans)
    send_vox = jnp.zeros((devices, slots), jnp.int32).at[owner, slot].set(point_voxel)
    got_feats, got_vox = (
        lax.all_to_all(send_feats, ("narrow", "region"), split_axis=0, concat_axis=0, tiled=True),
        lax.all_to_all(send_vox, ("narrow", "region"), split_axis=0, concat_axis=0, tiled=True),
    )
    incoming = got_feats.reshape(devices * slots, chans).astype(jnp.float32)
    targets = got_vox.reshape(devices * slots)
    sums = jax.ops.segment_sum(incoming, targets, num_segments=voxels)
    grid = sums.T.astype(jnp.bfloat16).reshape(chans, rows_x, CY, NZ)
    grads = cotangent.reshape(chans, rows_x, CY, NZ)
    padded = extended(grid, (("narrow", 2), ("region", 1)), 1)
    gpad = extended(grads, (("narrow", 2), ("region", 1)), 1)
    padded = jnp.pad(padded, ((0, 0), (0, 0), (0, 0), (1, 1)))
    stacked = stack_depth(padded, [0, 1, 2], NZ)
    gpad = jnp.pad(gpad, ((0, 0), (0, 0), (0, 0), (1, 1)))
    gstack = stack_depth(gpad, [2, 1, 0], NZ)
    flipped = weight.reshape(9, chans, 3, chans).transpose(0, 3, 2, 1).reshape(9, chans, 3 * chans)
    result = jnp.zeros((chans, rows_x, CY, NZ), jnp.float32)
    backward = jnp.zeros((chans, rows_x, CY, NZ), jnp.float32)
    kernels = []
    for a in range(3):
        for b in range(3):
            k = a * 3 + b
            window = stacked[:, a : a + rows_x, b : b + CY]
            result = result + jnp.einsum(
                "ok,kxyz->oxyz", weight[k], window, preferred_element_type=jnp.float32
            )
            kernels.append(
                jnp.einsum("oxyz,kxyz->ok", grads, window, preferred_element_type=jnp.float32)
            )
            backward = backward + jnp.einsum(
                "ck,kxyz->cxyz",
                flipped[k],
                gstack[:, 2 - a : 2 - a + rows_x, 2 - b : 2 - b + CY],
                preferred_element_type=jnp.float32,
            )
    conv_out = result.astype(jnp.bfloat16).reshape(chans, rows_x, CY * NZ)
    total_cells = rows_x * n_region * CY * n_narrow * NZ
    weight_grad = lax.psum(jnp.stack(kernels), ("narrow", "region")) * (
        1.0 / math.sqrt(total_cells)
    )
    grad_flat = backward.astype(jnp.bfloat16).reshape(chans, voxels)
    picked = jnp.take(grad_flat, targets, axis=1).T.reshape(devices, slots * chans)
    returned = lax.all_to_all(picked, ("narrow", "region"), split_axis=0, concat_axis=0, tiled=True)
    returned = returned.reshape(devices, slots, chans)
    point_grad = returned[owner, slot].T
    return (conv_out, point_grad, weight_grad)


def solution(mesh):
    in_specs = (
        P(None, ("narrow", "region")),
        P(("narrow", "region"), None),
        P(("narrow", "region")),
        P(),
        P(None, "region", "narrow"),
    )
    out_specs = (P(None, "region", "narrow"), P(None, ("narrow", "region")), P())
    return jax.shard_map(shards, mesh=mesh, in_specs=in_specs, out_specs=out_specs, check_vma=False)
```

profile of v0, /device:TPU:0, one launch (start us, length us, event | category | flops | bytes accessed | tf_op | source)
XLA Modules:
  0.0 687.5 jit_solution(5900122822803206030)
XLA Ops:
  7.9 9.2 %reduce-window.6 = s32[32,32,128]{2,1,0:T(8,128)S(1)} reduce-window(s32[32,32,128]{2,1,0:T(8,128)S(1)} %fusion.21, s32[]{:T(128)} %constant.14.clone.1), window={size=1x1x128 pad=0_0x0_0x127_0}, to_apply=%region_0.0 | reduce-window | flops 16646144 | bytes 1048580 | tf_op jit(solution)/shard_map/reduce-window
  21.8 16.3 %scatter_custom_fusion.1 = s32[8192]{0:T(1024)} fusion(s32[4096]{0:T(1024)S(1)} %broadcast_select_fusion.1, s32[4096]{0:T(1024)} %param.7, s32[]{:T(128)} %constant.14.clone.1), kind=kCustom, calls=%fused_computation.98 | custom fusion | bytes 33280
  38.1 7.4 %all-to-all-start = ((s32[32,1,256]{2,1,0:T(1,128)}), s32[32,1,256]{2,1,0:T(1,128)}, u32[]{:S(2)}, u32[]{:S(2)}) async-start(s32[32,1,256]{2,1,0:T(1,128)} %bitcast.5), calls=%async_computation | async-start | bytes 65536 | tf_op jit(solution)/shard_map/all_to_all | solution.py:48
  45.5 3.4 copy.56
  49.9 3.6 collective-permute-start.4
  58.5 2.4 copy.54
  60.9 12.9 %scatter_custom_fusion.2 = bf16[8192,64]{1,0:T(8,128)(2,1)} fusion(s32[4096]{0:T(1024)} %copy-done.17, bf16[4096,64]{1,0:T(8,128)(2,1)} %copy.54, bf16[]{:T(256)} %constant.33.clone.1), kind=kCustom, calls=%fused_computation.45 | custom fusion | bytes 1049088
  73.8 6.2 all_to_all.24
  80.6 9.4 %reduce.11 = bf16[32,16384]{1,0:T(8,128)(2,1)} reduce(bf16[32,1,16384]{2,1,0:T(2,128)(2,1)} %all_to_all.24, bf16[]{:T(256)} %broadcast.231), dimensions={1}, to_apply=%all_to_all.24.reduce_sub_computation | reduce | bytes 2097154 | tf_op jit(solution)/shard_map/all_to_all | solution.py:47
  89.9 2.6 reshape.224
  106.1 7.6 %all-to-all-start.1 = ((bf16[32,2,8192]{2,1,0:T(2,128)(2,1)}), bf16[32,2,8192]{2,1,0:T(2,128)(2,1)}, u32[]{:S(2)}, u32[]{:S(2)}) async-start(bf16[32,2,8192]{2,1,0:T(2,128)(2,1)} %reshape.224), calls=%async_computation.1 | async-start | bytes 2097152 | tf_op jit(solution)/shard_map/all_to_all | solution.py:47
  122.4 9.0 %select_maximum_fusion = bf16[64,26,10,66]{0,3,2,1:T(8,128)(2,1)S(1)} fusion(bf16[64,1,10,64]{0,3,2,1:T(8,128)(2,1)S(1)} %collective-permute-done.7, bf16[64,1,10,64]{0,3,2,1:T(8,128)(2,1)S(1)} %collective-permute-done.6, bf16[64,24,1,64]{0,3,2,1:T(8,128)(2,1)} %collective-permute-done.5, bf16[64,24,8,64]{0,3,2,1:T(8,128)(2,1)S(1)} %bitcast.265, ...), kind=kLoop, calls=%fused_computation.12 | loop fusion | flops 19768320 | bytes 4326400 | tf_op jit(solution)/shard_map/concatenate | solution.py:17
  131.4 2.4 fusion.50
  133.8 11.6 %pad_maximum_fusion.1 = bf16[192,26,10,64]{0,3,2,1:T(8,128)(2,1)S(1)} fusion(bf16[64,26,10,64]{0,3,2,1:T(8,128)(2,1)S(1)} %get-tuple-element.15, bf16[64,1,10,64]{0,3,2,1:T(8,128)(2,1)S(1)} %collective-permute-done.7, bf16[64,24,1,64]{0,3,2,1:T(8,128)(2,1)} %collective-permute-done.5, bf16[64,24,8,64]{0,3,2,1:T(8,128)(2,1)S(1)} %bitcast.266, ...), kind=kLoop, calls=%fused_computation.9 | loop fusion | flops 44728320 | bytes 12779520 | tf_op jit(solution)/shard_map/concatenate | solution.py:29
  145.4 4.4 fusion.55
  149.8 4.4 fusion.56
  154.3 4.4 fusion.57
  158.7 4.4 fusion.58
  163.0 4.5 fusion.59
  167.5 4.4 fusion.60
  171.9 4.4 fusion.61
  176.3 4.9 fusion.62
  181.2 18.4 %add_convert_fusion = bf16[24,8,64,64]{3,2,1,0:T(8,128)(2,1)} fusion(f32[24,8,64,64]{3,2,1,0:T(8,128)} %fusion.62, f32[24,8,64,64]{3,2,1,0:T(8,128)} %fusion.61, f32[24,8,64,64]{3,2,1,0:T(8,128)} %fusion.60, f32[24,8,64,64]{3,2,1,0:T(8,128)} %fusion.59, f32[24,8,64,64]{3,2,1,0:T(8,128)} %fusion.58, f32[24,8,64,64]{3,2,1,0:T(8,128)} %fusion.57, ...), kind=kOutput, calls=%fused_computation.10 | convolution fusion | flops 309067776 | bytes 33153024 | tf_op jit(solution)/shard_map/ck,kxyz->cxyz/dot_general | solution.py:75
  199.6 30.4 %gather_fusion = bf16[8192,64]{1,0:T(8,128)(2,1)} fusion(bf16[64,12288]{0,1:T(8,128)(2,1)} %bitcast.281, s32[8192]{0:T(1024)S(1)} %copy-done.15), kind=kCustom, calls=%fused_computation | custom fusion | bytes 2129920 | tf_op jit(solution)/shard_map/jit(_take)/gather | solution.py:87
  230.1 6.6 broadcast_select_fusion
  236.6 6.2 all_to_all.25
  242.8 9.4 %reduce.12 = bf16[32,16384]{1,0:T(8,128)(2,1)} reduce(bf16[32,1,16384]{2,1,0:T(2,128)(2,1)} %all_to_all.25, bf16[]{:T(256)} %broadcast.231), dimensions={1}, to_apply=%all_to_all.25.reduce_sub_computation | reduce | bytes 2097154 | tf_op jit(solution)/shard_map/all_to_all | solution.py:88
  252.2 2.6 reshape.226
  254.8 21.9 %all-to-all-start.2 = ((bf16[32,2,8192]{2,1,0:T(2,128)(2,1)}), bf16[32,2,8192]{2,1,0:T(2,128)(2,1)}, u32[]{:S(2)}, u32[]{:S(2)}) async-start(bf16[32,2,8192]{2,1,0:T(2,128)(2,1)} %reshape.226), calls=%async_computation.2 | async-start | bytes 2097152 | tf_op jit(solution)/shard_map/all_to_all | solution.py:88
  276.8 5.9 reshape.225
  282.7 9.0 %convert_reduce_fusion = f32[32,16384]{1,0:T(8,128)} fusion(bf16[32,1,16384]{2,1,0:T(2,128)(2,1)} %reshape.225), kind=kLoop, calls=%fused_computation.25 | loop fusion | flops 524288 | bytes 3145728 | tf_op jit(solution)/shard_map/convert_element_type | solution.py:50
  291.7 4.3 reshape.171
  296.0 52.3 %scatter_custom_fusion = f32[12288,64]{1,0:T(8,128)} fusion(s32[8192]{0:T(1024)} %bitcast.6, f32[8192,64]{1,0:T(8,128)} %reshape.171, f32[]{:T(128)} %constant.13.clone.1), kind=kCustom, calls=%fused_computation.23 | custom fusion | flops 524288 | bytes 3146240 | tf_op jit(solution)/shard_map/scatter-add | solution.py:52
  348.3 3.0 convert_element_type.29
  351.4 8.3 %collective-permute-start = (bf16[64,24,1,64]{0,3,2,1:T(8,128)(2,1)S(1)}, bf16[64,24,1,64]{0,3,2,1:T(8,128)(2,1)S(1)}, u32[]{:S(2)}, u32[]{:S(2)}) collective-permute-start(bf16[64,24,1,64]{0,3,2,1:T(8,128)(2,1)S(1)} %get-tuple-element.24), channel_id=1, source_target_pairs={{0,8},{8,16},{16,24},{1,9},{9,17},{17,25},{2,10},{10,18},{18,26},{... | collective-permute-start | bytes 589832 | tf_op jit(solution)/shard_map/ppermute | solution.py:19
  361.1 4.0 collective-permute-done
  365.0 5.9 collective-permute-done.1
  375.1 6.2 reshape.227
  381.3 8.7 %reduce.6 = bf16[32,16384]{1,0:T(8,128)(2,1)} reduce(bf16[32,1,16384]{2,1,0:T(2,128)(2,1)} %reshape.227, bf16[]{:T(256)} %constant.72), dimensions={1}, to_apply=%all_to_all.23.reduce_sub_computation | reduce | bytes 2097154 | tf_op jit(solution)/shard_map/all_to_all | solution.py:88
  390.0 4.0 reshape.141
  394.0 67.6 %gather_fusion.1 = bf16[4096,64]{1,0:T(8,128)(2,1)} fusion(bf16[32,256,64]{2,1,0:T(8,128)(2,1)} %reshape.141, s32[4096]{0:T(1024)S(1)} %bitcast.276), kind=kCustom, calls=%fused_computation.1 | custom fusion | bytes 1081344 | tf_op jit(solution)/shard_map/gather | solution.py:90
  461.6 2.3 copy.87
  464.0 9.6 %select_maximum_fusion.4 = bf16[64,26,10,66]{0,3,2,1:T(8,128)(2,1)S(1)} fusion(bf16[64,1,10,64]{0,3,2,1:T(8,128)(2,1)} %collective-permute-done.3, bf16[64,1,10,64]{0,3,2,1:T(8,128)(2,1)} %collective-permute-done.2, bf16[64,24,1,64]{0,3,2,1:T(8,128)(2,1)} %copy-done.3, bf16[64,24,8,64]{0,3,2,1:T(8,128)(2,1)} %bitcast.279, ...), kind=kLoop, calls=%fused_computation.16 | loop fusion | flops 19768320 | bytes 4326400 | tf_op jit(solution)/shard_map/concatenate | solution.py:17
  473.6 2.3 fusion.51
  475.9 11.3 %pad_maximum_fusion = bf16[192,26,10,64]{0,3,2,1:T(8,128)(2,1)S(1)} fusion(bf16[64,26,10,64]{0,3,2,1:T(8,128)(2,1)S(1)} %get-tuple-element.17, bf16[64,1,10,64]{0,3,2,1:T(8,128)(2,1)} %collective-permute-done.3, bf16[64,24,1,64]{0,3,2,1:T(8,128)(2,1)S(1)} %copy-done.4, bf16[64,24,8,64]{0,3,2,1:T(8,128)(2,1)S(1)} %bitcast.280, ...), kind=kLoop, calls=%fused_computation.8 | loop fusion | flops 44728320 | bytes 12779520 | tf_op jit(solution)/shard_map/concatenate | solution.py:29
  487.2 2.8 fusion.16
  490.0 4.5 fusion.23
  494.4 4.3 fusion.25
  498.8 4.4 fusion.27
  503.2 4.4 fusion.29
  507.6 4.4 fusion.31
  512.0 4.3 fusion.33
  516.3 4.4 fusion.35
  520.7 4.6 fusion.37
  527.4 2.1 fusion.14
  529.5 2.1 fusion.13
  531.7 2.1 fusion.12
  533.8 2.1 fusion.11
  535.9 2.1 fusion.10
  538.0 2.1 fusion.9
  540.2 2.1 fusion.8
  542.3 18.5 %add_convert_fusion.1 = bf16[24,8,64,64]{3,2,1,0:T(8,128)(2,1)S(1)} fusion(f32[24,8,64,64]{3,2,1,0:T(8,128)} %fusion.23, f32[24,8,64,64]{3,2,1,0:T(8,128)} %fusion.25, f32[24,8,64,64]{3,2,1,0:T(8,128)} %fusion.27, f32[24,8,64,64]{3,2,1,0:T(8,128)} %fusion.29, f32[24,8,64,64]{3,2,1,0:T(8,128)} %fusion.31, f32[24,8,64,64]{3,2,1,0:T(8,128)} %fusion.33, ...), kind=kOutput, calls=%fused_computation.11 | convolution fusion | flops 309067776 | bytes 33161216 | tf_op jit(solution)/shard_map/ok,kxyz->oxyz/dot_general | solution.py:69
  560.8 3.1 copy.86
  564.0 114.5 %all-reduce.4.cloned.1.call-done = f32[9,64,192]{2,1,0:T(8,128)} async-done(((f32[9,64,192]{2,1,0:T(8,128)}), f32[9,64,192]{2,1,0:T(8,128)}) %all-reduce.4.cloned.1.call-update) | async-done | bytes 442384 | tf_op jit(solution)/shard_map/psum | solution.py:83
  (84 shorter events, 43.8 us)
Async XLA Ops:
  21.8 16.3 %copy-start.17 = (s32[4096]{0:T(1024)}, s32[4096]{0:T(1024)S(1)}, u32[]{:S(2)}) copy-start(s32[4096]{0:T(1024)S(1)} %broadcast_select_fusion.1) | copy-start | bytes 49156
  38.1 68.0 %all-to-all-start = ((s32[32,1,256]{2,1,0:T(1,128)}), s32[32,1,256]{2,1,0:T(1,128)}, u32[]{:S(2)}, u32[]{:S(2)}) async-start(s32[32,1,256]{2,1,0:T(1,128)} %bitcast.5), calls=%async_computation | async-start | bytes 65536 | tf_op jit(solution)/shard_map/all_to_all | solution.py:48
  49.9 65.2 %collective-permute-start.4 = (bf16[64,24,1,64]{0,3,2,1:T(8,128)(2,1)}, bf16[64,24,1,64]{0,3,2,1:T(8,128)(2,1)S(1)}, u32[]{:S(2)}, u32[]{:S(2)}) collective-permute-start(bf16[64,24,1,64]{0,3,2,1:T(8,128)(2,1)} %get-tuple-element.22), channel_id=1, source_target_pairs={{0,8},{8,16},{16,24},{1,9},{9,17},{17,25},{2,10},{10,18},{18,26},{... | collective-permute-start | bytes 589832 | tf_op jit(solution)/shard_map/ppermute | solution.py:19
  53.5 61.6 %collective-permute-start.5 = (bf16[64,24,1,64]{0,3,2,1:T(8,128)(2,1)}, bf16[64,24,1,64]{0,3,2,1:T(8,128)(2,1)}, u32[]{:S(2)}, u32[]{:S(2)}) collective-permute-start(bf16[64,24,1,64]{0,3,2,1:T(8,128)(2,1)} %get-tuple-element.23), channel_id=1, source_target_pairs={{8,0},{16,8},{24,16},{9,1},{17,9},{25,17},{10,2},{18,10},{26,18},{... | collective-permute-start | bytes 589832 | tf_op jit(solution)/shard_map/ppermute | solution.py:21
  106.1 148.8 %all-to-all-start.1 = ((bf16[32,2,8192]{2,1,0:T(2,128)(2,1)}), bf16[32,2,8192]{2,1,0:T(2,128)(2,1)}, u32[]{:S(2)}, u32[]{:S(2)}) async-start(bf16[32,2,8192]{2,1,0:T(2,128)(2,1)} %reshape.224), calls=%async_computation.1 | async-start | bytes 2097152 | tf_op jit(solution)/shard_map/all_to_all | solution.py:47
  115.9 4.8 collective-permute-start.6
  118.0 4.4 collective-permute-start.7
  133.7 11.6 %copy-start.7 = (bf16[1,64,3,64]{1,3,2,0:T(8,128)(2,1)S(1)}, bf16[1,64,3,64]{1,3,2,0:T(8,128)(2,1)}, u32[]{:S(2)}) copy-start(bf16[1,64,3,64]{1,3,2,0:T(8,128)(2,1)} %copy.58) | copy-start | bytes 73732
  145.4 4.5 copy-start.8
  149.8 4.4 copy-start.9
  154.3 4.4 copy-start.10
  158.6 4.4 copy-start.11
  163.0 4.5 copy-start.12
  167.5 4.4 copy-start.13
  171.9 4.4 copy-start.14
  176.3 4.9 copy-start.6
  181.2 18.4 %copy-start.15 = (s32[8192]{0:T(1024)S(1)}, s32[8192]{0:T(1024)}, u32[]{:S(2)}) copy-start(s32[8192]{0:T(1024)} %broadcast_clamp_fusion) | copy-start | bytes 98308
  199.6 30.4 %copy-start.16 = (pred[8192]{0:T(1024)(128)(4,1)S(1)}, pred[8192]{0:T(1024)(128)(4,1)}, u32[]{:S(2)}) copy-start(pred[8192]{0:T(1024)(128)(4,1)} %compare_and_fusion) | copy-start | bytes 24580
  254.8 120.2 %all-to-all-start.2 = ((bf16[32,2,8192]{2,1,0:T(2,128)(2,1)}), bf16[32,2,8192]{2,1,0:T(2,128)(2,1)}, u32[]{:S(2)}, u32[]{:S(2)}) async-start(bf16[32,2,8192]{2,1,0:T(2,128)(2,1)} %reshape.226), calls=%async_computation.2 | async-start | bytes 2097152 | tf_op jit(solution)/shard_map/all_to_all | solution.py:88
  276.8 401.7 %all-reduce.4.cloned.1.call-start = ((), (), s32[]{:S(2)}) async-start(), calls=%async_computation.3 | async-start | bytes 1179648 | tf_op jit(solution)/shard_map/psum | solution.py:83
  351.4 19.6 %copy-start.1 = (bf16[12288,64]{1,0:T(8,128)(2,1)}, bf16[12288,64]{1,0:T(8,128)(2,1)S(1)}, u32[]{:S(2)}) copy-start(bf16[12288,64]{1,0:T(8,128)(2,1)S(1)} %convert_element_type.29) | copy-start | bytes 4718596
  351.4 13.6 %collective-permute-start = (bf16[64,24,1,64]{0,3,2,1:T(8,128)(2,1)S(1)}, bf16[64,24,1,64]{0,3,2,1:T(8,128)(2,1)S(1)}, u32[]{:S(2)}, u32[]{:S(2)}) collective-permute-start(bf16[64,24,1,64]{0,3,2,1:T(8,128)(2,1)S(1)} %get-tuple-element.24), channel_id=1, source_target_pairs={{0,8},{8,16},{16,24},{1,9},{9,17},{17,25},{2,10},{10,18},{18,26},{... | collective-permute-start | bytes 589832 | tf_op jit(solution)/shard_map/ppermute | solution.py:19
  359.8 11.2 %collective-permute-start.1 = (bf16[64,24,1,64]{0,3,2,1:T(8,128)(2,1)S(1)}, bf16[64,24,1,64]{0,3,2,1:T(8,128)(2,1)S(1)}, u32[]{:S(2)}, u32[]{:S(2)}) collective-permute-start(bf16[64,24,1,64]{0,3,2,1:T(8,128)(2,1)S(1)} %get-tuple-element.25), channel_id=1, source_target_pairs={{8,0},{16,8},{24,16},{9,1},{17,9},{25,17},{10,2},{18,10},{26,18},{... | collective-permute-start | bytes 589832 | tf_op jit(solution)/shard_map/ppermute | solution.py:21
  370.9 0.9 copy-start.3
  371.8 92.2 %collective-permute-start.2 = (bf16[64,1,10,64]{0,3,2,1:T(8,128)(2,1)}, bf16[64,1,10,64]{0,3,2,1:T(8,128)(2,1)}, u32[]{:S(2)}, u32[]{:S(2)}) collective-permute-start(bf16[64,1,10,64]{0,3,2,1:T(8,128)(2,1)} %get-tuple-element.20), channel_id=1, source_target_pairs={{0,1},{1,2},{2,3},{3,4},{4,5},{5,6},{6,7},{8,9},{9,10},{10,11},{11... | collective-permute-start | bytes 245768 | tf_op jit(solution)/shard_map/ppermute | solution.py:19
  373.8 90.2 %collective-permute-start.3 = (bf16[64,1,10,64]{0,3,2,1:T(8,128)(2,1)}, bf16[64,1,10,64]{0,3,2,1:T(8,128)(2,1)}, u32[]{:S(2)}, u32[]{:S(2)}) collective-permute-start(bf16[64,1,10,64]{0,3,2,1:T(8,128)(2,1)} %get-tuple-element.21), channel_id=1, source_target_pairs={{1,0},{2,1},{3,2},{4,3},{5,4},{6,5},{7,6},{9,8},{10,9},{11,10},{12... | collective-permute-start | bytes 245768 | tf_op jit(solution)/shard_map/ppermute | solution.py:21
  473.5 2.4 copy-start.2
  473.6 2.4 copy-start.4
  487.2 53.0 %copy-start = (bf16[192,26,10,64]{0,3,2,1:T(8,128)(2,1)}, bf16[192,26,10,64]{0,3,2,1:T(8,128)(2,1)S(1)}, u32[]{:S(2)}) copy-start(bf16[192,26,10,64]{0,3,2,1:T(8,128)(2,1)S(1)} %pad_maximum_fusion) | copy-start | bytes 19169284
  487.2 2.8 copy-start.5
Sparse Core Ops, SparseCore 0:
  542.4 135.9 all-reduce.3
where the time goes:
time: 696 us; the launch traced here: 687 us
  local copies, waits for them, and re-layouts  201 us (29%)
  other arithmetic  160 us (23%)
  matrix products  128 us (18%)
  waiting for transfers between devices  126 us (18%)
  starting transfers between devices  58.1 us (8%)
  between operations  14.6 us (2%)
    psum x1, waiting for transfers between devices, shards(): lax.psum(jnp.stack(kernels), ('narrow', 'region'))  114 us
    gather x1, local copies, waits for them, and re-layouts, shards(): point_grad = returned[owner, slot].T  67.6 us
    unnamed x46, local copies, waits for them, and re-layouts  57.5 us
    dot_general x9, matrix products, shards(): jnp.einsum('ck,kxyz->cxyz', flipped[k], gstack[:, 2 - a:2 - a + rows_x, 2...  54.2 us
    dot_general x9, matrix products, shards(): jnp.einsum('ok,kxyz->oxyz', weight[k], window, preferred_element_type=jnp...  53.8 us
    scatter-add x1, other arithmetic, shards(): sums = jax.ops.segment_sum(incoming, targets, num_segments=voxels)  52.3 us
    gather x1, local copies, waits for them, and re-layouts, shards(): jnp.take(grad_flat, targets, axis=1).T.reshape(devices, slots * chans)  30.4 us
    concatenate x2, other arithmetic, stack_depth(): return jnp.concatenate([padded[..., o:o + depth] for o in offsets], axis=0)  22.9 us
  transfers between devices with their start and end apart: 12, of which 4 were waited for; matrix products, arithmetic and copies ran while one was open for 53% of the time, Pallas kernels for 0%

commit v1 on v0

--- a/solution.py
+++ b/solution.py
@@ -80,7 +80,7 @@
             )
     conv_out = result.astype(jnp.bfloat16).reshape(chans, rows_x, CY * NZ)
     total_cells = rows_x * n_region * CY * n_narrow * NZ
-    weight_grad = lax.psum(jnp.stack(kernels), ("narrow", "region")) * (
+    weight_grad = jnp.sum(lax.all_gather(jnp.stack(kernels), ("narrow", "region")), axis=0) * (
         1.0 / math.sqrt(total_cells)
     )
     grad_flat = backward.astype(jnp.bfloat16).reshape(chans, voxels)

time: 696 us -> 568 us (0.82)
  waiting for transfers between devices: 126 us -> 26.8 us
  local copies, waits for them, and re-layouts: 201 us -> 134 us
  blocking collectives: 0 us -> 40.5 us
  starting transfers between devices: 58.1 us -> 49.9 us
    psum x1 -> x0, waiting for transfers between devices: 114 us -> none  [shards(): lax.psum(jnp.stack(kernels), ('narrow', 'region'))]
    gather x1, local copies, waits for them, and re-layouts: 67.6 us -> 22 us  [shards(): point_grad = returned[owner, slot].T]
    all_to_all x0 -> x1, blocking collectives: none -> 40.5 us  [shards(): lax.all_to_all(picked, ('narrow', 'region'), split_axis=0, concat_axis=0,...]
    all_to_all x1 -> x0, starting transfers between devices: 21.9 us -> none  [shards(): lax.all_to_all(picked, ('narrow', 'region'), split_axis=0, concat_axis=0,...]
    ppermute x4, starting transfers between devices: 5.16 us -> 18 us  [extended(): lax.ppermute(head, axis, [((i + 1) % count, i) for i in range(ends)])]
    unnamed x46 -> x52, local copies, waits for them, and re-layouts: 57.5 us -> 46.1 us
    all_to_all x1, waiting for transfers between devices: 0.01 us -> 11.3 us  [shards(): lax.all_to_all(send_feats, ('narrow', 'region'), split_axis=0, concat_axi...]
    reduce_sum x0 -> x1, other arithmetic: none -> 8.19 us  [shards(): jnp.sum(lax.all_gather(jnp.stack(kernels), ('narrow', 'region')), axis=0)]
  transfers between devices with their start and end apart: 12 -> 11, of which waited for: 4 -> 5; matrix products, arithmetic and copies ran while one was open for 53% -> 49% of each run, Pallas kernels for 0% -> 0%
where the time goes in v1:
time: 568 us; the launch traced here: 558 us
  other arithmetic  161 us (28%)
  local copies, waits for them, and re-layouts  134 us (24%)
  matrix products  131 us (23%)
  starting transfers between devices  49.9 us (9%)
  blocking collectives  40.5 us (7%)
  waiting for transfers between devices  26.8 us (5%)
  between operations  15 us (3%)
    dot_general x9, matrix products, shards(): jnp.einsum('ok,kxyz->oxyz', weight[k], window, preferred_element_type=jnp...  59.6 us
    dot_general x9, matrix products, shards(): jnp.einsum('ck,kxyz->cxyz', flipped[k], gstack[:, 2 - a:2 - a + rows_x, 2...  52.4 us
    scatter-add x1, other arithmetic, shards(): sums = jax.ops.segment_sum(incoming, targets, num_segments=voxels)  52.4 us
    unnamed x52, local copies, waits for them, and re-layouts  46.1 us
    all_to_all x1, blocking collectives, shards(): lax.all_to_all(picked, ('narrow', 'region'), split_axis=0, concat_axis=0,...  40.5 us
    gather x1, local copies, waits for them, and re-layouts, shards(): jnp.take(grad_flat, targets, axis=1).T.reshape(devices, slots * chans)  29.4 us
    concatenate x2, other arithmetic, stack_depth(): return jnp.concatenate([padded[..., o:o + depth] for o in offsets], axis=0)  22.5 us
    gather x1, local copies, waits for them, and re-layouts, shards(): point_grad = returned[owner, slot].T  22 us
  transfers between devices with their start and end apart: 11, of which 5 were waited for; matrix products, arithmetic and copies ran while one was open for 49% of the time, Pallas kernels for 0%

profile of v1, /device:TPU:0, one launch (start us, length us, event | category | flops | bytes accessed | tf_op | source)
XLA Modules:
  0.0 558.0 jit_solution(3888486853055913269)
XLA Ops:
  7.9 9.2 %reduce-window.6 = s32[32,32,128]{2,1,0:T(8,128)S(1)} reduce-window(s32[32,32,128]{2,1,0:T(8,128)S(1)} %fusion.21, s32[]{:T(128)} %constant.14.clone.1), window={size=1x1x128 pad=0_0x0_0x127_0}, to_apply=%region_0.0 | reduce-window | flops 16646144 | bytes 1048580 | tf_op jit(solution)/shard_map/reduce-window
  23.9 11.6 %scatter_custom_fusion.2 = bf16[8192,64]{1,0:T(8,128)(2,1)S(1)} fusion(s32[4096]{0:T(1024)S(1)} %broadcast_select_fusion.1, bf16[4096,64]{1,0:T(8,128)(2,1)S(1)} %copy.54, bf16[]{:T(256)} %constant.34.clone.1), kind=kCustom, calls=%fused_computation.45 | custom fusion | bytes 1048578
  35.5 3.6 all_to_all.24
  39.7 8.4 %reduce.11 = bf16[32,16384]{1,0:T(8,128)(2,1)S(1)} reduce(bf16[32,1,16384]{2,1,0:T(2,128)(2,1)} %all_to_all.24, bf16[]{:T(256)} %broadcast.231), dimensions={1}, to_apply=%all_to_all.24.reduce_sub_computation | reduce | bytes 2097154 | tf_op jit(solution)/shard_map/all_to_all | solution.py:47
  49.7 7.6 %all-to-all-start.1 = ((bf16[32,2,8192]{2,1,0:T(2,128)(2,1)}), bf16[32,2,8192]{2,1,0:T(2,128)(2,1)S(1)}, u32[]{:S(2)}, u32[]{:S(2)}) async-start(bf16[32,2,8192]{2,1,0:T(2,128)(2,1)} %reshape.225), calls=%async_computation.1 | async-start | bytes 2097152 | tf_op jit(solution)/shard_map/all_to_all | solution.py:47
  57.3 16.3 %scatter_custom_fusion.1 = s32[8192]{0:T(1024)} fusion(s32[4096]{0:T(1024)S(1)} %broadcast_select_fusion.1, s32[4096]{0:T(1024)} %param.7, s32[]{:T(128)} %constant.14.clone.1), kind=kCustom, calls=%fused_computation.98 | custom fusion | bytes 33280
  73.6 11.3 %all-to-all-done.1 = bf16[32,2,8192]{2,1,0:T(2,128)(2,1)S(1)} async-done(((bf16[32,2,8192]{2,1,0:T(2,128)(2,1)}), bf16[32,2,8192]{2,1,0:T(2,128)(2,1)S(1)}, u32[]{:S(2)}, u32[]{:S(2)}) %all-to-all-start.1) | async-done | bytes 1048608 | tf_op jit(solution)/shard_map/all_to_all | solution.py:47
  84.9 2.6 all-to-all-start
  87.5 3.5 reshape.226
  90.9 7.7 %convert_reduce_fusion = f32[32,16384]{1,0:T(8,128)S(1)} fusion(bf16[32,1,16384]{2,1,0:T(2,128)(2,1)} %reshape.226), kind=kLoop, calls=%fused_computation.25 | loop fusion | flops 524288 | bytes 3145728 | tf_op jit(solution)/shard_map/convert_element_type | solution.py:50
  98.6 3.1 reshape.171
  101.7 52.4 %scatter_custom_fusion = f32[12288,64]{1,0:T(8,128)} fusion(s32[8192]{0:T(1024)S(1)} %bitcast.291, f32[8192,64]{1,0:T(8,128)} %reshape.171, f32[]{:T(128)} %constant.13.clone.1), kind=kCustom, calls=%fused_computation.23 | custom fusion | flops 524288 | bytes 3146240 | tf_op jit(solution)/shard_map/scatter-add | solution.py:52
  154.1 3.0 convert_element_type.29
  157.2 8.3 %collective-permute-start = (bf16[64,24,1,64]{0,3,2,1:T(8,128)(2,1)S(1)}, bf16[64,24,1,64]{0,3,2,1:T(8,128)(2,1)S(1)}, u32[]{:S(2)}, u32[]{:S(2)}) collective-permute-start(bf16[64,24,1,64]{0,3,2,1:T(8,128)(2,1)S(1)} %get-tuple-element.24), channel_id=1, source_target_pairs={{0,8},{8,16},{16,24},{1,9},{9,17},{17,25},{2,10},{10,18},{18,26},{... | collective-permute-start | bytes 589832 | tf_op jit(solution)/shard_map/ppermute | solution.py:19
  166.7 4.0 collective-permute-done
  170.7 5.9 %collective-permute-done.1 = bf16[64,24,1,64]{0,3,2,1:T(8,128)(2,1)S(1)} collective-permute-done((bf16[64,24,1,64]{0,3,2,1:T(8,128)(2,1)S(1)}, bf16[64,24,1,64]{0,3,2,1:T(8,128)(2,1)S(1)}, u32[]{:S(2)}, u32[]{:S(2)}) %collective-permute-start.1) | collective-permute-done | bytes 196640 | tf_op jit(solution)/shard_map/ppermute | solution.py:21
  179.4 14.1 %collective-permute-start.3 = (bf16[64,1,10,64]{0,3,2,1:T(8,128)(2,1)}, bf16[64,1,10,64]{0,3,2,1:T(8,128)(2,1)}, u32[]{:S(2)}, u32[]{:S(2)}) collective-permute-start(bf16[64,1,10,64]{0,3,2,1:T(8,128)(2,1)} %get-tuple-element.21), channel_id=1, source_target_pairs={{1,0},{2,1},{3,2},{4,3},{5,4},{6,5},{7,6},{9,8},{10,9},{11,10},{12... | collective-permute-start | bytes 245768 | tf_op jit(solution)/shard_map/ppermute | solution.py:21
  193.6 3.4 copy.56
  197.0 9.6 %select_maximum_fusion.4 = bf16[64,26,10,66]{0,3,2,1:T(8,128)(2,1)S(1)} fusion(bf16[64,1,10,64]{0,3,2,1:T(8,128)(2,1)} %collective-permute-done.3, bf16[64,1,10,64]{0,3,2,1:T(8,128)(2,1)} %collective-permute-done.2, bf16[64,24,1,64]{0,3,2,1:T(8,128)(2,1)} %copy-done.4, bf16[64,24,8,64]{0,3,2,1:T(8,128)(2,1)} %bitcast.282, ...), kind=kLoop, calls=%fused_computation.16 | loop fusion | flops 19768320 | bytes 4326400 | tf_op jit(solution)/shard_map/concatenate | solution.py:17
  206.6 2.3 fusion.51
  209.0 11.1 %pad_maximum_fusion = bf16[192,26,10,64]{0,3,2,1:T(8,128)(2,1)S(1)} fusion(bf16[64,26,10,64]{0,3,2,1:T(8,128)(2,1)S(1)} %get-tuple-element.17, bf16[64,1,10,64]{0,3,2,1:T(8,128)(2,1)} %collective-permute-done.3, bf16[64,24,1,64]{0,3,2,1:T(8,128)(2,1)S(1)} %copy-done.5, bf16[64,24,8,64]{0,3,2,1:T(8,128)(2,1)S(1)} %bitcast.283, ...), kind=kLoop, calls=%fused_computation.8 | loop fusion | flops 44728320 | bytes 12779520 | tf_op jit(solution)/shard_map/concatenate | solution.py:29
  220.1 2.6 fusion.16
  222.7 2.1 fusion.15
  224.7 2.0 fusion.14
  226.8 2.1 fusion.13
  228.8 2.0 fusion.12
  230.9 2.1 fusion.11
  235.0 2.1 fusion.9
  237.0 2.1 fusion.8
  240.0 9.1 %collective-permute-start.4 = (bf16[64,24,1,64]{0,3,2,1:T(8,128)(2,1)}, bf16[64,24,1,64]{0,3,2,1:T(8,128)(2,1)S(1)}, u32[]{:S(2)}, u32[]{:S(2)}) collective-permute-start(bf16[64,24,1,64]{0,3,2,1:T(8,128)(2,1)} %get-tuple-element.22), channel_id=1, source_target_pairs={{0,8},{8,16},{16,24},{1,9},{9,17},{17,25},{2,10},{10,18},{18,26},{... | collective-permute-start | bytes 589832 | tf_op jit(solution)/shard_map/ppermute | solution.py:19
  269.0 2.6 collective-permute-done.5
  272.5 2.4 collective-permute-start.6
  277.0 2.9 collective-permute-done.7
  279.9 9.4 %select_maximum_fusion = bf16[64,26,10,66]{0,3,2,1:T(8,128)(2,1)S(1)} fusion(bf16[64,1,10,64]{0,3,2,1:T(8,128)(2,1)S(1)} %collective-permute-done.7, bf16[64,1,10,64]{0,3,2,1:T(8,128)(2,1)S(1)} %collective-permute-done.6, bf16[64,24,1,64]{0,3,2,1:T(8,128)(2,1)} %collective-permute-done.5, bf16[64,24,8,64]{0,3,2,1:T(8,128)(2,1)S(1)} %bitcast.277, ...), kind=kLoop, calls=%fused_computation.12 | loop fusion | flops 19768320 | bytes 4326400 | tf_op jit(solution)/shard_map/concatenate | solution.py:17
  289.3 2.4 fusion.50
  291.6 11.4 %pad_maximum_fusion.1 = bf16[192,26,10,64]{0,3,2,1:T(8,128)(2,1)S(1)} fusion(bf16[64,26,10,64]{0,3,2,1:T(8,128)(2,1)S(1)} %get-tuple-element.15, bf16[64,1,10,64]{0,3,2,1:T(8,128)(2,1)S(1)} %collective-permute-done.7, bf16[64,24,1,64]{0,3,2,1:T(8,128)(2,1)} %collective-permute-done.5, bf16[64,24,8,64]{0,3,2,1:T(8,128)(2,1)S(1)} %bitcast.278, ...), kind=kLoop, calls=%fused_computation.9 | loop fusion | flops 44728320 | bytes 12779520 | tf_op jit(solution)/shard_map/concatenate | solution.py:29
  303.1 4.4 fusion.55
  307.5 4.4 fusion.56
  311.9 4.4 fusion.57
  316.2 4.4 fusion.58
  320.6 4.4 fusion.59
  325.0 4.5 fusion.60
  329.5 4.4 fusion.61
  334.0 4.5 fusion.62
  338.5 17.0 %add_convert_fusion = bf16[24,8,64,64]{3,2,1,0:T(8,128)(2,1)S(1)} fusion(f32[24,8,64,64]{3,2,1,0:T(8,128)} %fusion.62, f32[24,8,64,64]{3,2,1,0:T(8,128)} %fusion.61, f32[24,8,64,64]{3,2,1,0:T(8,128)} %fusion.60, f32[24,8,64,64]{3,2,1,0:T(8,128)} %fusion.59, f32[24,8,64,64]{3,2,1,0:T(8,128)} %fusion.58, f32[24,8,64,64]{3,2,1,0:T(8,128)} %fusion.57, ...), kind=kOutput, calls=%fused_computation.10 | convolution fusion | flops 309067776 | bytes 33153024 | tf_op jit(solution)/shard_map/ck,kxyz->cxyz/dot_general | solution.py:75
  355.5 29.4 %gather_fusion = bf16[8192,64]{1,0:T(8,128)(2,1)} fusion(bf16[64,12288]{0,1:T(8,128)(2,1)S(1)} %bitcast.284, s32[8192]{0:T(1024)S(1)} %copy-done.17), kind=kCustom, calls=%fused_computation | custom fusion | bytes 2129920 | tf_op jit(solution)/shard_map/jit(_take)/gather | solution.py:87
  385.0 5.8 %broadcast_select_fusion = bf16[8192,64]{1,0:T(8,128)(2,1)S(1)} fusion(bf16[8192,64]{1,0:T(8,128)(2,1)} %gather_fusion, pred[8192]{0:T(1024)(128)(4,1)S(1)} %compare_and_fusion), kind=kLoop, calls=%fused_computation.26 | loop fusion | flops 524288 | bytes 2105344 | tf_op jit(solution)/shard_map/jit(_take)/select_n | solution.py:87
  390.8 3.7 all_to_all.25
  394.4 8.4 %reduce.12 = bf16[32,16384]{1,0:T(8,128)(2,1)S(1)} reduce(bf16[32,1,16384]{2,1,0:T(2,128)(2,1)} %all_to_all.25, bf16[]{:T(256)} %broadcast.231), dimensions={1}, to_apply=%all_to_all.25.reduce_sub_computation | reduce | bytes 2097154 | tf_op jit(solution)/shard_map/all_to_all | solution.py:88
  403.7 40.5 %all_to_all.29 = bf16[32,2,8192]{2,1,0:T(2,128)(2,1)S(1)} all-to-all(bf16[32,2,8192]{2,1,0:T(2,128)(2,1)S(1)} %reshape.227), channel_id=1, replica_groups=mesh['narrow'=4,'region'=8] {'narrow','region'}, dimensions={0} | all-to-all | bytes 2097152 | tf_op jit(solution)/shard_map/all_to_all | solution.py:88
  445.3 6.4 %reduce.6 = bf16[32,16384]{1,0:T(8,128)(2,1)S(1)} reduce(bf16[32,1,16384]{2,1,0:T(2,128)(2,1)S(1)} %reshape.228, bf16[]{:T(256)} %constant.73), dimensions={1}, to_apply=%all_to_all.23.reduce_sub_computation | reduce | bytes 2097154 | tf_op jit(solution)/shard_map/all_to_all | solution.py:88
  451.7 2.3 reshape.141
  454.0 22.0 %gather_fusion.1 = bf16[4096,64]{1,0:T(8,128)(2,1)S(1)} fusion(bf16[32,256,64]{2,1,0:T(8,128)(2,1)S(1)} %reshape.141, s32[4096]{0:T(1024)S(1)} %bitcast.279), kind=kCustom, calls=%fused_computation.1 | custom fusion | bytes 1081344 | tf_op jit(solution)/shard_map/gather | solution.py:90
  477.1 7.3 %fusion.23 = f32[24,8,64,64]{3,2,1,0:T(8,128)} fusion(bf16[192,26,10,64]{0,3,2,1:T(8,128)(2,1)} %copy-done, bf16[9,64,192]{2,1,0:T(8,128)(2,1)S(1)} %copy-done.6), kind=kOutput, calls=%fused_computation.69 | convolution fusion | flops 301989888 | bytes 9568256 | tf_op jit(solution)/shard_map/ok,kxyz->oxyz/dot_general | solution.py:69
  484.4 7.2 %fusion.25 = f32[24,8,64,64]{3,2,1,0:T(8,128)} fusion(bf16[192,26,10,64]{0,3,2,1:T(8,128)(2,1)} %copy-done, bf16[9,64,192]{2,1,0:T(8,128)(2,1)S(1)} %copy-done.6), kind=kOutput, calls=%fused_computation.71 | convolution fusion | flops 301989888 | bytes 9568256 | tf_op jit(solution)/shard_map/ok,kxyz->oxyz/dot_general | solution.py:69
  491.7 4.4 fusion.27
  496.1 4.3 fusion.29
  500.4 4.4 fusion.31
  504.8 4.4 fusion.33
  509.2 4.4 fusion.35
  513.6 4.5 fusion.37
  518.1 18.7 %add_convert_fusion.1 = bf16[24,8,64,64]{3,2,1,0:T(8,128)(2,1)} fusion(f32[24,8,64,64]{3,2,1,0:T(8,128)} %fusion.23, f32[24,8,64,64]{3,2,1,0:T(8,128)} %fusion.25, f32[24,8,64,64]{3,2,1,0:T(8,128)} %fusion.27, f32[24,8,64,64]{3,2,1,0:T(8,128)} %fusion.29, f32[24,8,64,64]{3,2,1,0:T(8,128)} %fusion.31, f32[24,8,64,64]{3,2,1,0:T(8,128)} %fusion.33, ...), kind=kOutput, calls=%fused_computation.11 | convolution fusion | flops 309067776 | bytes 35291136 | tf_op jit(solution)/shard_map/ok,kxyz->oxyz/dot_general | solution.py:69
  536.8 4.8 copy.86
  541.6 8.2 %reduce_sum.19 = f32[9,64,192]{2,1,0:T(8,128)S(1)} reduce(f32[32,9,64,192]{3,2,1,0:T(8,128)} %bitcast.285, f32[]{:T(128)} %constant.13.clone.1), dimensions={0}, to_apply=%region_6.7 | reduce | flops 3428352 | bytes 14598148 | tf_op jit(solution)/shard_map/reduce_sum | solution.py:83
  (91 shorter events, 43.5 us)
Async XLA Ops:
  49.7 35.1 %all-to-all-start.1 = ((bf16[32,2,8192]{2,1,0:T(2,128)(2,1)}), bf16[32,2,8192]{2,1,0:T(2,128)(2,1)S(1)}, u32[]{:S(2)}, u32[]{:S(2)}) async-start(bf16[32,2,8192]{2,1,0:T(2,128)(2,1)} %reshape.225), calls=%async_computation.1 | async-start | bytes 2097152 | tf_op jit(solution)/shard_map/all_to_all | solution.py:47
  84.9 16.9 %all-to-all-start = ((s32[32,1,256]{2,1,0:T(1,128)}), s32[32,1,256]{2,1,0:T(1,128)S(1)}, u32[]{:S(2)}, u32[]{:S(2)}) async-start(s32[32,1,256]{2,1,0:T(1,128)} %bitcast.5), calls=%async_computation | async-start | bytes 65536 | tf_op jit(solution)/shard_map/all_to_all | solution.py:48
  87.4 454.2 %all-gather.3.cloned.1.call-start = ((), (), s32[]{:S(2)}) async-start(), calls=%async_computation.3 | async-start | bytes 19464192 | tf_op jit(solution)/shard_map/all_gather | solution.py:83
  101.7 55.4 %copy-start.7 = (s32[32,1,256]{2,1,0:T(1,128)}, s32[32,1,256]{2,1,0:T(1,128)S(1)}, u32[]{:S(2)}) copy-start(s32[32,1,256]{2,1,0:T(1,128)S(1)} %all-to-all-done) | copy-start | bytes 98308
  157.1 22.3 %copy-start.2 = (bf16[12288,64]{1,0:T(8,128)(2,1)}, bf16[12288,64]{1,0:T(8,128)(2,1)S(1)}, u32[]{:S(2)}) copy-start(bf16[12288,64]{1,0:T(8,128)(2,1)S(1)} %convert_element_type.29) | copy-start | bytes 4718596
  157.2 13.5 %collective-permute-start = (bf16[64,24,1,64]{0,3,2,1:T(8,128)(2,1)S(1)}, bf16[64,24,1,64]{0,3,2,1:T(8,128)(2,1)S(1)}, u32[]{:S(2)}, u32[]{:S(2)}) collective-permute-start(bf16[64,24,1,64]{0,3,2,1:T(8,128)(2,1)S(1)} %get-tuple-element.24), channel_id=1, source_target_pairs={{0,8},{8,16},{16,24},{1,9},{9,17},{17,25},{2,10},{10,18},{18,26},{... | collective-permute-start | bytes 589832 | tf_op jit(solution)/shard_map/ppermute | solution.py:19
  165.4 11.2 %collective-permute-start.1 = (bf16[64,24,1,64]{0,3,2,1:T(8,128)(2,1)S(1)}, bf16[64,24,1,64]{0,3,2,1:T(8,128)(2,1)S(1)}, u32[]{:S(2)}, u32[]{:S(2)}) collective-permute-start(bf16[64,24,1,64]{0,3,2,1:T(8,128)(2,1)S(1)} %get-tuple-element.25), channel_id=1, source_target_pairs={{8,0},{16,8},{24,16},{9,1},{17,9},{25,17},{10,2},{18,10},{26,18},{... | collective-permute-start | bytes 589832 | tf_op jit(solution)/shard_map/ppermute | solution.py:21
  176.6 2.8 copy-start.4
  177.5 19.5 %collective-permute-start.2 = (bf16[64,1,10,64]{0,3,2,1:T(8,128)(2,1)}, bf16[64,1,10,64]{0,3,2,1:T(8,128)(2,1)}, u32[]{:S(2)}, u32[]{:S(2)}) collective-permute-start(bf16[64,1,10,64]{0,3,2,1:T(8,128)(2,1)} %get-tuple-element.20), channel_id=1, source_target_pairs={{0,1},{1,2},{2,3},{3,4},{4,5},{5,6},{6,7},{8,9},{9,10},{10,11},{11... | collective-permute-start | bytes 245768 | tf_op jit(solution)/shard_map/ppermute | solution.py:19
  179.4 17.6 %collective-permute-start.3 = (bf16[64,1,10,64]{0,3,2,1:T(8,128)(2,1)}, bf16[64,1,10,64]{0,3,2,1:T(8,128)(2,1)}, u32[]{:S(2)}, u32[]{:S(2)}) collective-permute-start(bf16[64,1,10,64]{0,3,2,1:T(8,128)(2,1)} %get-tuple-element.21), channel_id=1, source_target_pairs={{1,0},{2,1},{3,2},{4,3},{5,4},{6,5},{7,6},{9,8},{10,9},{11,10},{12... | collective-permute-start | bytes 245768 | tf_op jit(solution)/shard_map/ppermute | solution.py:21
  206.6 2.4 copy-start.3
  206.6 2.4 copy-start.5
  220.0 17.0 %copy-start = (bf16[192,26,10,64]{0,3,2,1:T(8,128)(2,1)}, bf16[192,26,10,64]{0,3,2,1:T(8,128)(2,1)S(1)}, u32[]{:S(2)}) copy-start(bf16[192,26,10,64]{0,3,2,1:T(8,128)(2,1)S(1)} %pad_maximum_fusion) | copy-start | bytes 19169284
  240.0 29.0 %collective-permute-start.4 = (bf16[64,24,1,64]{0,3,2,1:T(8,128)(2,1)}, bf16[64,24,1,64]{0,3,2,1:T(8,128)(2,1)S(1)}, u32[]{:S(2)}, u32[]{:S(2)}) collective-permute-start(bf16[64,24,1,64]{0,3,2,1:T(8,128)(2,1)} %get-tuple-element.22), channel_id=1, source_target_pairs={{0,8},{8,16},{16,24},{1,9},{9,17},{17,25},{2,10},{10,18},{18,26},{... | collective-permute-start | bytes 589832 | tf_op jit(solution)/shard_map/ppermute | solution.py:19
  249.1 22.5 %collective-permute-start.5 = (bf16[64,24,1,64]{0,3,2,1:T(8,128)(2,1)}, bf16[64,24,1,64]{0,3,2,1:T(8,128)(2,1)}, u32[]{:S(2)}, u32[]{:S(2)}) collective-permute-start(bf16[64,24,1,64]{0,3,2,1:T(8,128)(2,1)} %get-tuple-element.23), channel_id=1, source_target_pairs={{8,0},{16,8},{24,16},{9,1},{17,9},{25,17},{10,2},{18,10},{26,18},{... | collective-permute-start | bytes 589832 | tf_op jit(solution)/shard_map/ppermute | solution.py:21
  272.5 4.5 collective-permute-start.6
  274.9 5.0 collective-permute-start.7
  291.6 11.4 %copy-start.9 = (bf16[1,64,3,64]{1,3,2,0:T(8,128)(2,1)S(1)}, bf16[1,64,3,64]{1,3,2,0:T(8,128)(2,1)}, u32[]{:S(2)}) copy-start(bf16[1,64,3,64]{1,3,2,0:T(8,128)(2,1)} %copy.58) | copy-start | bytes 73732
  303.1 4.4 copy-start.10
  307.5 4.4 copy-start.11
  311.9 4.4 copy-start.12
  316.2 4.4 copy-start.13
  320.6 4.4 copy-start.14
  325.0 4.5 copy-start.15
  329.5 4.4 copy-start.16
  334.0 4.5 copy-start.8
  338.5 17.0 %copy-start.17 = (s32[8192]{0:T(1024)S(1)}, s32[8192]{0:T(1024)}, u32[]{:S(2)}) copy-start(s32[8192]{0:T(1024)} %broadcast_clamp_fusion) | copy-start | bytes 98308
  403.7 50.3 %copy-start.1 = (s32[4096,1]{0,1:T(1,128)S(1)}, s32[4096,1]{0,1:T(1,128)}, u32[]{:S(2)}) copy-start(s32[4096,1]{0,1:T(1,128)} %get-tuple-element.12) | copy-start | bytes 49156
  454.0 23.1 %copy-start.6 = (bf16[9,64,192]{2,1,0:T(8,128)(2,1)S(1)}, bf16[9,64,192]{2,1,0:T(8,128)(2,1)}, u32[]{:S(2)}) copy-start(bf16[9,64,192]{2,1,0:T(8,128)(2,1)} %param.8) | copy-start | bytes 663556
  477.1 14.6 %slice-start = ((s8[8519680]{0:T(1024)(128)(4,1)}), s8[4194304]{0:T(1024)(128)(4,1)S(1)}, s32[]{:S(2)}) async-start(s8[8519680]{0:T(1024)(128)(4,1)} %bitcast.264), calls=%async_computation.4 | async-start | bytes 8388608
  477.1 14.6 %slice-start.1 = ((s8[8519680]{0:T(1024)(128)(4,1)}), s8[4194304]{0:T(1024)(128)(4,1)S(1)}, s32[]{:S(2)}) async-start(s8[8519680]{0:T(1024)(128)(4,1)} %bitcast.264), calls=%async_computation.5 | async-start | bytes 8388608
  484.4 7.2 %slice-start.2 = ((s8[8519680]{0:T(1024)(128)(4,1)}), s8[131072]{0:T(1024)(128)(4,1)S(1)}, s32[]{:S(2)}) async-start(s8[8519680]{0:T(1024)(128)(4,1)} %bitcast.264), calls=%async_computation.6 | async-start | bytes 262144
Sparse Core Ops, SparseCore 0:
  239.2 136.3 all-gather.2
